TPU v7x, 128 devices: a whole 4x4x4 slice. The times are simulated.
128 devices in a mesh: req: 4 (over x), hid: 32 (over y, z, core).
Axes of the slice: x: 4, y: 4, z: 4, core: 2. Of those that a mesh axis runs over, the one named last changes fastest.
Arguments:
- layer_input: bfloat16 [2048, 7168], P('req', 'hid'), may hold values from -6 to 6
- norm_gain: float32 [7168], replicated, may hold values from 0.1 to 1.9
- qkv_weight: bfloat16 [7168, 21504], P('req', 'hid'), may hold values from -0.09375 to 0.09375
- cache_keys: bfloat16 [4, 4096, 7168], P('req', None, 'hid'), may hold values from -160 to 160
- cache_values: bfloat16 [4, 4096, 7168], P('req', None, 'hid'), may hold values from -8 to 8
- cache_lengths: int32 [4], P('req'), may hold values from 1 to 4096, 10240 in all
- out_weight: bfloat16 [7168, 3584], P('hid'), may hold values from -0.375 to 0.375
- mlp_gain: float32 [3584], replicated, may hold values from 0.1 to 1.9
- gate_weight: bfloat16 [3584, 14336], P(None, 'hid'), may hold values from -0.09375 to 0.09375
- up_weight: bfloat16 [3584, 14336], P(None, 'hid'), may hold values from -0.09375 to 0.09375
- down_weight: bfloat16 [14336, 3584], P('hid'), may hold values from -0.046875 to 0.046875
Outputs:
- block_out: bfloat16 [2048, 3584], P(('req', 'hid'))
All inputs are finite; a program needn't handle non-finite values. No bound on the sum of `cache_lengths` on one device may be relied on, other than what follows from the above.
Results may differ from a plain program's by a relative error of at most 0.02.
Values may be sent and summed in bfloat16 or wider, within the bound.
A program may use at most 128 MiB of HBM per device.

v0:
```python
import jax
import jax.numpy as jnp
from jax import lax
from jax.sharding import PartitionSpec as P

D = 3584
HD = 224


epsilon = 1e-05


def rms_scale(values, gain):
    return values * lax.rsqrt(jnp.mean(values * values, axis=-1, keepdims=True) + epsilon) * gain


def rotate(values, position):
    half = values.shape[-1] // 2
    freq = jnp.exp(-jnp.log(10000.0) * 2.0 * jnp.arange(half, dtype=jnp.float32) / values.shape[-1])
    angle = position.astype(jnp.float32)[:, None, None] * freq[None, None, :]
    cosine = jnp.cos(angle)
    sine = jnp.sin(angle)
    first = values[..., :half]
    second = values[..., half:]
    return jnp.concatenate(
        [first * cosine - second * sine, second * cosine + first * sine], axis=-1
    )


def merge_block(carry, scores, values):
    top, total, accum = carry
    new_top = jnp.maximum(top, jnp.max(scores, axis=2))
    fade = jnp.exp(top - new_top)
    weights = jnp.exp(scores - new_top[:, :, None])
    total = total * fade + jnp.sum(weights, axis=2)
    accum = accum * fade.T[:, :, None] + jnp.einsum(
        "hqk,khd->qhd", weights.astype(jnp.bfloat16), values, preferred_element_type=jnp.float32
    )
    return (new_top, total, accum)


def shards(
    layer_input,
    norm_gain,
    qkv_weight,
    cache_keys,
    cache_values,
    cache_lengths,
    out_weight,
    mlp_gain,
    gate_weight,
    up_weight,
    down_weight,
):
    span = layer_input.shape[0]
    heads_dev = cache_keys.shape[2] // HD
    slots = cache_keys.shape[1]
    scale = HD ** (-0.5)
    whole_input = lax.all_gather(layer_input, "hid", axis=1, tiled=True)
    normed = rms_scale(whole_input.astype(jnp.float32), norm_gain).astype(jnp.bfloat16)
    columns = normed
    projected = jnp.dot(
        columns,
        lax.all_gather(qkv_weight, "req", axis=0, tiled=True),
        preferred_element_type=jnp.float32,
    ).reshape(span, heads_dev, 3, HD)
    length = cache_lengths[0]
    position = length + jnp.arange(span, dtype=jnp.int32)
    query = rotate(projected[:, :, 0], position).astype(jnp.bfloat16)
    fresh_keys = rotate(projected[:, :, 1], position).astype(jnp.bfloat16)
    fresh_values = projected[:, :, 2].astype(jnp.bfloat16)
    cache_k = cache_keys[0].reshape(slots, heads_dev, HD)
    cache_v = cache_values[0].reshape(slots, heads_dev, HD)
    block = min(512, slots)
    block_count = (length + block - 1) // block

    def visit(index, carry):
        keys = lax.dynamic_slice_in_dim(cache_k, index * block, block, 0)
        values = lax.dynamic_slice_in_dim(cache_v, index * block, block, 0)
        scores = jnp.einsum("qhd,khd->hqk", query, keys, preferred_element_type=jnp.float32) * scale
        columns = index * block + jnp.arange(block, dtype=jnp.int32)
        scores = jnp.where(columns[None, None, :] < length, scores, -1e30)
        return merge_block(carry, scores, values)

    start_state = (
        jnp.full((heads_dev, span), -1e30, jnp.float32),
        jnp.zeros((heads_dev, span), jnp.float32),
        jnp.zeros((span, heads_dev, HD), jnp.float32),
    )
    state = lax.fori_loop(0, block_count, visit, start_state)
    fresh_scores = (
        jnp.einsum("qhd,khd->hqk", query, fresh_keys, preferred_element_type=jnp.float32) * scale
    )
    causal = (
        jnp.arange(span, dtype=jnp.int32)[None, :] <= jnp.arange(span, dtype=jnp.int32)[:, None]
    )
    fresh_scores = jnp.where(causal[None, :, :], fresh_scores, -1e30)
    top, total, accum = merge_block(state, fresh_scores, fresh_values)
    heads_out = (accum / total.T[:, :, None]).astype(jnp.bfloat16).reshape(span, heads_dev * HD)
    row_count = span // lax.axis_size("hid")
    row_start = lax.axis_index("hid") * row_count
    attention = lax.psum(
        jnp.dot(heads_out, out_weight, preferred_element_type=jnp.float32).astype(jnp.bfloat16),
        "hid",
    ).astype(jnp.float32)
    mid = (whole_input[:, :D].astype(jnp.float32) + attention).astype(jnp.bfloat16)
    mlp_in = rms_scale(mid.astype(jnp.float32), mlp_gain).astype(jnp.bfloat16)
    gate = jnp.dot(mlp_in, gate_weight, preferred_element_type=jnp.float32)
    upward = jnp.dot(mlp_in, up_weight, preferred_element_type=jnp.float32)
    hidden = (jax.nn.gelu(gate, approximate=True) * upward).astype(jnp.bfloat16)
    mlp_part = lax.psum_scatter(
        jnp.dot(hidden, down_weight, preferred_element_type=jnp.float32).astype(jnp.bfloat16),
        "hid",
        scatter_dimension=0,
        tiled=True,
    ).astype(jnp.float32)
    mid_own = lax.dynamic_slice_in_dim(mid, row_start, row_count, 0)
    return (mid_own.astype(jnp.float32) + mlp_part).astype(jnp.bfloat16)


def solution(mesh):
    placed = (
        P("req", "hid"),
        P(),
        P("req", "hid"),
        P("req", None, "hid"),
        P("req", None, "hid"),
        P("req"),
        P("hid", None),
        P(),
        P(None, "hid"),
        P(None, "hid"),
        P("hid", None),
    )
    return jax.shard_map(
        shards, mesh=mesh, in_specs=placed, out_specs=P(("req", "hid"), None), check_vma=False
    )
```

profile of v0, /device:TPU:2, one launch (start us, length us, event | category | flops | bytes accessed | tf_op | source)
XLA Modules:
  0.0 435.7 jit_solution(8863642717574515305)
XLA Ops:
  8.8 54.1 %all-gather.3.cloned.1.call-done = bf16[512,7168]{0,1:T(8,128)(2,1)} async-done(((bf16[512,224]{0,1:T(8,128)(2,1)}), bf16[512,7168]{0,1:T(8,128)(2,1)}) %all-gather.3.cloned.1.call-update) | async-done | bytes 7340048 | tf_op jit(solution)/shard_map/all_gather | solution.py:59
  62.9 4.7 %fusion.13 = f32[512]{0:T(512)S(1)} fusion(bf16[512,7168]{0,1:T(8,128)(2,1)} %all-gather.3.cloned.1.call-done), kind=kLoop, calls=%fused_computation.20 | loop fusion | flops 11009536 | bytes 7342080 | tf_op jit(solution)/shard_map/reduce_sum | solution.py:14
  67.6 89.6 %all-gather.5.cloned.1.call-done = bf16[7168,672]{0,1:T(8,128)(2,1)} async-done(((bf16[1792,672]{0,1:T(8,128)(2,1)}), bf16[7168,672]{0,1:T(8,128)(2,1)}) %all-gather.5.cloned.1.call-update) | async-done | bytes 9633808 | tf_op jit(solution)/shard_map/all_gather | solution.py:64
  157.2 11.0 %fusion.19 = f32[512,672]{0,1:T(8,128)S(1)} fusion(bf16[7168,672]{0,1:T(8,128)(2,1)} %all-gather.5.cloned.1.call-done, bf16[512,7168]{0,1:T(8,128)(2,1)} %all-gather.3.cloned.1.call-done, f32[7168]{0:T(1024)S(1)} %copy-done.5, f32[512]{0:T(512)S(1)} %add_rsqrt_fusion.1), kind=kOutput, calls=%fused_computation.28 | convolution fusion | flops 4947181568 | bytes 18380800 | tf_op jit(solution)/shard_map/dot_general | solution.py:62
  168.3 1.7 fusion.78
  171.6 27.8 %while.14 = (s32[]{:T(128)}, f32[1,512]{1,0:T(1,128)S(1)}, f32[1,512]{1,0:T(1,128)S(1)}, f32[512,1,224]{0,2,1:T(8,128)}, s32[]{:T(128)}, /*index=5*/s32[]{:T(128...) while((s32[]{:T(128)}, f32[1,512]{1,0:T(1,128)S(1)}, ...), condition=%wide.region_4.5_spmd, body=%wide.region_1.4_spmd.sunk | while | flops 236947456 | bytes 4785347 | solution.py:90
  173.9 2.3 fusion.96
  176.9 1.4 fusion.94
  178.5 2.3 fusion.96
  183.1 2.3 fusion.96
  187.8 2.3 fusion.96
  192.4 2.3 fusion.96
  195.4 1.4 fusion.94
  197.0 2.3 fusion.96
  201.9 5.3 %convolution_convert_fusion = bf16[512,3584]{1,0:T(8,128)(2,1)} fusion(bf16[224,3584]{1,0:T(8,128)(2,1)} %param.19, f32[512,512]{0,1:T(8,128)} %copy-done.1, f32[512]{0:T(512)S(1)} %bitcast.98, f32[512,1,224]{0,2,1:T(8,128)} %get-tuple-element.55, f32[512,1,3,224]{0,3,2,1:T(8,128)} %bitcast.88, f32[512]{0:T(512)S(1)} %bitcast.100, f32[512]{0:T(512)S(1)} %bitcast.101), kind=kOutput, calls=%fused_computation.32 | convolution fusion | flops 942342144 | bytes 7018496 | tf_op jit(solution)/shard_map/dot_general | solution.py:103
  207.5 4.1 slice.33
  211.6 5.9 %copy.21 = bf16[512,3584]{1,0:T(8,128)(2,1)} copy(bf16[512,3584]{0,1:T(8,128)(2,1)} %slice.33) | data formatting | bytes 7340032
  217.5 109.9 %all-reduce.2.cloned.1.call-done = bf16[512,3584]{1,0:T(8,128)(2,1)} async-done(((bf16[512,3584]{1,0:T(8,128)(2,1)}), bf16[512,3584]{1,0:T(8,128)(2,1)}) %all-reduce.2.cloned.1.call-update) | async-done | bytes 3670032 | tf_op jit(solution)/shard_map/psum | solution.py:102
  327.4 4.9 %fusion.16 = (f32[512]{0:T(512)S(1)}, bf16[512,3584]{1,0:T(8,128)(2,1)S(1)}) fusion(bf16[512,3584]{1,0:T(8,128)(2,1)} %all-reduce.2.cloned.1.call-done, bf16[512,3584]{1,0:T(8,128)(2,1)} %copy.21), kind=kLoop, calls=%fused_computation.25 | loop fusion | flops 12844544 | bytes 11012096 | tf_op jit(solution)/shard_map/reduce_sum | solution.py:14
  332.3 1.8 copy-done.2
  334.1 3.1 fusion.40
  337.2 9.0 %convolution_convert_fusion.1 = bf16[512,3584]{1,0:T(8,128)(2,1)} fusion(bf16[448,3584]{1,0:T(8,128)(2,1)S(1)} %copy-done, f32[512,448]{0,1:T(8,128)} %fusion.40, bf16[3584,448]{0,1:T(8,128)(2,1)} %param.22, bf16[512,3584]{1,0:T(8,128)(2,1)} %copy-done.2, f32[3584]{0:T(1024)S(1)} %copy-done.6, f32[512]{0:T(512)S(1)} %add_rsqrt_fusion), kind=kOutput, calls=%fused_computation.33 | convolution fusion | flops 3297968128 | bytes 14696448 | tf_op jit(solution)/shard_map/dot_general | solution.py:112
  346.2 81.4 %reduce-scatter.2.cloned.1.call-done = bf16[16,3584]{1,0:T(8,128)(2,1)} async-done(((bf16[512,3584]{1,0:T(8,128)(2,1)}), bf16[16,3584]{1,0:T(8,128)(2,1)}) %reduce-scatter.2.cloned.1.call-update) | async-done | bytes 114704 | tf_op jit(solution)/shard_map/reduce_scatter | solution.py:111
  427.6 1.6 add_convert_fusion.1
  (68 shorter events, 16.8 us)
Async XLA Ops:
  6.5 330.6 %copy-start = (bf16[448,3584]{1,0:T(8,128)(2,1)S(1)}, bf16[448,3584]{1,0:T(8,128)(2,1)}, u32[]{:S(2)}) copy-start(bf16[448,3584]{1,0:T(8,128)(2,1)} %param.23) | copy-start | bytes 9633796
  6.5 56.4 %all-gather.3.cloned.1.call-start = ((), (), s32[]{:S(2)}) async-start(), calls=%async_computation.1 | async-start | bytes 7569408 | tf_op jit(solution)/shard_map/all_gather | solution.py:59
  7.3 149.9 %all-gather.5.cloned.1.call-start = ((), (), s32[]{:S(2)}) async-start(), calls=%async_computation.2 | async-start | bytes 12042240 | tf_op jit(solution)/shard_map/all_gather | solution.py:64
  8.0 319.4 %all-reduce.2.cloned.1.call-start = ((), (), s32[]{:S(2)}) async-start(), calls=%async_computation.3 | async-start | bytes 7340032 | tf_op jit(solution)/shard_map/psum | solution.py:102
  8.7 148.4 %copy-start.5 = (f32[7168]{0:T(1024)S(1)}, f32[7168]{0:T(1024)}, u32[]{:S(2)}) copy-start(f32[7168]{0:T(1024)} %param.14) | copy-start | bytes 86020
  168.2 1.8 copy-start.3
  200.7 1.0 copy-start.1
  207.3 220.3 %reduce-scatter.2.cloned.1.call-start = ((), (), s32[]{:S(2)}) async-start(), calls=%async_computation.4 | async-start | bytes 3784704 | tf_op jit(solution)/shard_map/reduce_scatter | solution.py:111
  217.5 116.6 %copy-start.6 = (f32[3584]{0:T(1024)S(1)}, f32[3584]{0:T(1024)}, u32[]{:S(2)}) copy-start(f32[3584]{0:T(1024)} %param.20) | copy-start | bytes 43012
  327.4 6.7 %copy-start.4 = (bf16[3584,448]{0,1:T(8,128)(2,1)S(1)}, bf16[3584,448]{0,1:T(8,128)(2,1)}, u32[]{:S(2)}) copy-start(bf16[3584,448]{0,1:T(8,128)(2,1)} %param.21) | copy-start | bytes 9633796
  332.3 1.8 copy-start.2
Sparse Core Ops, SparseCore 0:
  9.6 53.2 all-gather.2
  64.6 92.5 all-gather.4
  207.4 119.9 all-reduce.1
  346.3 81.1 reduce-scatter.1
where the time goes:
time: 437 us; the launch traced here: 436 us
  waiting for transfers between devices  336 us (77%)
  matrix products  52.2 us (12%)
  other arithmetic  19 us (4%)
  between operations  13.9 us (3%)
  local copies, waits for them, and re-layouts  13.8 us (3%)
    psum x1, waiting for transfers between devices, shards(): lax.psum(jnp.dot(heads_out, out_weight, preferred_element_type=jnp.float3...  110 us
    all_gather x1, waiting for transfers between devices, shards(): lax.all_gather(qkv_weight, 'req', axis=0, tiled=True)  89.6 us
    reduce_scatter x1, waiting for transfers between devices, shards(): lax.psum_scatter(jnp.dot(hidden, down_weight, preferred_element_type=jnp....  81.4 us
    all_gather x1, waiting for transfers between devices, shards(): whole_input = lax.all_gather(layer_input, 'hid', axis=1, tiled=True)  54.1 us
    dot_general x6, matrix products, merge_block(): jnp.einsum('hqk,khd->qhd', weights.astype(jnp.bfloat16), values, preferre...  14 us
    dot_general x1, matrix products, shards(): jnp.dot(columns, lax.all_gather(qkv_weight, 'req', axis=0, tiled=True), p...  11 us
    reduce_sum x2, other arithmetic, rms_scale(): jnp.mean(values * values, axis=-1, keepdims=True) + epsilon  9.55 us
    dot_general x1, matrix products, shards(): jnp.dot(hidden, down_weight, preferred_element_type=jnp.float32)  8.99 us
  transfers between devices with their start and end apart: 4, of which 4 were waited for; matrix products, arithmetic and copies ran while one was open for 3% of the time, Pallas kernels for 0%

commit v1 on v0

--- a/solution.py
+++ b/solution.py
@@ -1,17 +1,292 @@
 import jax
 import jax.numpy as jnp
 from jax import lax
+from jax.experimental import pallas as pl
+from jax.experimental.pallas import tpu as pltpu
 from jax.sharding import PartitionSpec as P
 
 D = 3584
 HD = 224
-
-
+MESH = pl.DeviceIdType.MESH
 epsilon = 1e-05
+F32 = jnp.float32
+BF16 = jnp.bfloat16
+CHUNKS = 4
+CW = D // CHUNKS
+HALF = D // 2
 
 
 def rms_scale(values, gain):
     return values * lax.rsqrt(jnp.mean(values * values, axis=-1, keepdims=True) + epsilon) * gain
+
+
+class Net:
+    def __init__(self, send_sems, recv_sems):
+        self.send_sems, self.recv_sems, self.used = send_sems, recv_sems, 0
+        self.started = []
+
+    def copy(self, src, dst, device):
+        n = self.used
+        self.used += 1
+        op = pltpu.make_async_remote_copy(
+            src_ref=src,
+            dst_ref=dst,
+            send_sem=self.send_sems.at[n],
+            recv_sem=self.recv_sems.at[n],
+            device_id=device,
+            device_id_type=MESH,
+        )
+        op.start()
+        self.started.append(op)
+        return op
+
+    def drain(self):
+        for op in self.started:
+            op.wait_send()
+        self.started = []
+
+
+def ring(value, step):
+    return (value + step) % 4
+
+
+def place():
+    row = lax.axis_index("req")
+    hid = lax.axis_index("hid")
+    return row, hid // 8, (hid // 2) % 4, hid % 2
+
+
+def reduce_scatter(net, partial, bufs):
+    row, y, z, c = place()
+    out_ref, in_ref, s_ref, t1_ref, t2_ref, s1_ref, t3_ref = bufs
+
+    def first_axis(k, pos):
+        return (row, pos * 8 + z * 2 + c) if k % 2 == 0 else (row, y * 8 + pos * 2 + c)
+
+    def second_axis(k, pos):
+        return (row, y * 8 + pos * 2 + c) if k % 2 == 0 else (row, pos * 8 + z * 2 + c)
+
+    pair = []
+    for k in range(CHUNKS):
+        out_ref[k] = partial(1 - c, k).astype(BF16)
+        pair.append(net.copy(out_ref.at[k], in_ref.at[k], (row, y * 8 + z * 2 + 1 - c)))
+    relay = []
+    straight = []
+    for k in range(CHUNKS):
+        u = y if k % 2 == 0 else z
+        mine = partial(c, k)
+        pair[k].wait_recv()
+        total = (mine + in_ref[k].astype(F32)).astype(BF16)
+        for a in range(4):
+            for b in range(4):
+                rows = total[(a * 4 + b) * 16 : (a * 4 + b + 1) * 16]
+                if k % 2 == 0:
+                    s_ref[k, a, b] = rows
+                else:
+                    s_ref[k, b, a] = rows
+        far, near = [], []
+        for way in range(2):
+            nb = ring(u, 1 if way == 0 else 3)
+            ha, hb = (0, 2) if way == 0 else (2, 0)
+            target = first_axis(k, nb)
+            far.append(net.copy(s_ref.at[k, ring(u, 2), pl.ds(ha, 2)], t1_ref.at[k, way], target))
+            near.append(net.copy(s_ref.at[k, nb, pl.ds(hb, 2)], t2_ref.at[k, way, pl.ds(hb, 2)], target))
+        relay.append(far)
+        straight.append(near)
+    closing = []
+    for k in range(CHUNKS):
+        u = y if k % 2 == 0 else z
+        ends = []
+        for way in range(2):
+            nb = ring(u, 1 if way == 0 else 3)
+            ha = 0 if way == 0 else 2
+            relay[k][way].wait_recv()
+            s_ref[k, nb, pl.ds(ha, 2)] = (
+                s_ref[k, nb, pl.ds(ha, 2)].astype(F32) + t1_ref[k, way].astype(F32)
+            ).astype(BF16)
+            ends.append(
+                net.copy(s_ref.at[k, nb, pl.ds(ha, 2)], t2_ref.at[k, way, pl.ds(ha, 2)], first_axis(k, nb))
+            )
+        closing.append(ends)
+    last = []
+    for k in range(CHUNKS):
+        u, w = (y, z) if k % 2 == 0 else (z, y)
+        for way in range(2):
+            straight[k][way].wait_recv()
+            closing[k][way].wait_recv()
+        s1_ref[k] = (
+            s_ref[k, u].astype(F32) + t2_ref[k, 0].astype(F32) + t2_ref[k, 1].astype(F32)
+        ).astype(BF16)
+        sends = []
+        for step in range(1, 4):
+            peer = ring(w, step)
+            sends.append(net.copy(s1_ref.at[k, peer], t3_ref.at[k, step - 1], second_axis(k, peer)))
+        last.append(sends)
+    result = []
+    for k in range(CHUNKS):
+        w = z if k % 2 == 0 else y
+        value = s1_ref[k, w].astype(F32)
+        for step in range(3):
+            last[k][step].wait_recv()
+            value = value + t3_ref[k, step].astype(F32)
+        result.append(value)
+    return jnp.concatenate(result, axis=1)
+
+
+def all_gather(net, m_ref):
+    row, y, z, c = place()
+    here = m_ref.at[y, z, c]
+    first = []
+    for half in range(2):
+        cols = pl.ds(half * HALF, HALF)
+        sends = []
+        for step in range(1, 4):
+            device = (row, y * 8 + ring(z, step) * 2 + c) if half == 0 else (row, ring(y, step) * 8 + z * 2 + c)
+            sends.append(net.copy(here.at[:, cols], here.at[:, cols], device))
+        first.append(sends)
+
+    def block(half, u, lo, count):
+        cols = pl.ds(half * HALF, HALF)
+        if half == 0:
+            return m_ref.at[u, pl.ds(lo, count), c, :, cols]
+        return m_ref.at[pl.ds(lo, count), u, c, :, cols]
+
+    def device(half, u):
+        return (row, u * 8 + z * 2 + c) if half == 0 else (row, y * 8 + u * 2 + c)
+
+    partner = (row, y * 8 + z * 2 + 1 - c)
+    near, far, swap = [], [], []
+    for half in range(2):
+        u = y if half == 0 else z
+        for op in first[half]:
+            op.wait_recv()
+        near.append([net.copy(block(half, u, 0, 4), block(half, u, 0, 4), device(half, ring(u, s))) for s in (1, 3)])
+    for half in range(2):
+        u = y if half == 0 else z
+        swap.append(net.copy(block(half, u, 0, 4), block(half, u, 0, 4), partner))
+    for half in range(2):
+        u = y if half == 0 else z
+        ends = []
+        for way in range(2):
+            near[half][way].wait_recv()
+            source = ring(u, 3 if way == 0 else 1)
+            lo = 0 if way == 0 else 2
+            ends.append(
+                net.copy(
+                    block(half, source, lo, 2), block(half, source, lo, 2), device(half, ring(u, 1 if way == 0 else 3))
+                )
+            )
+            swap.append(net.copy(block(half, source, 0, 4), block(half, source, 0, 4), partner))
+        far.append(ends)
+    for half in range(2):
+        u = y if half == 0 else z
+        for op in far[half]:
+            op.wait_recv()
+        swap.append(net.copy(block(half, ring(u, 2), 0, 4), block(half, ring(u, 2), 0, 4), partner))
+    for op in swap:
+        op.wait_recv()
+
+
+def post_kernel(
+    heads_hbm, x_hbm, shift_hbm, ow_hbm, gain_ref, gw_hbm, uw_hbm, dw_hbm,
+    out_ref,
+    heads, x, shift, ow, gw, uw, dw, m_ref, hidden,
+    p_out, p_in, s_ref, t1, t2, s1, t3,
+    send_sems, recv_sems, local_sems,
+):
+    row, y, z, c = place()
+    loads = []
+    for n, (src, dst) in enumerate(
+        [(heads_hbm, heads), (ow_hbm, ow), (x_hbm, x), (shift_hbm, shift), (gw_hbm, gw), (uw_hbm, uw), (dw_hbm, dw)]
+    ):
+        op = pltpu.make_async_copy(src, dst, local_sems.at[n])
+        op.start()
+        loads.append(op)
+    barrier = pltpu.get_barrier_semaphore()
+    peers = [(row, y * 8 + z * 2 + 1 - c)]
+    for step in range(1, 4):
+        peers.append((row, ring(y, step) * 8 + z * 2 + c))
+        peers.append((row, y * 8 + ring(z, step) * 2 + c))
+    for peer in peers:
+        pl.semaphore_signal(barrier, inc=1, device_id=peer, device_id_type=MESH)
+    pl.semaphore_wait(barrier, len(peers))
+
+    net = Net(send_sems, recv_sems)
+    for n in range(4):
+        loads[n].wait()
+
+    def bufs(n):
+        return tuple(ref.at[n] for ref in (p_out, p_in, s_ref, t1, t2, s1, t3))
+
+    def attention_part(core, k):
+        cols = pl.ds(k * CW, CW)
+        return jnp.dot(
+            heads[:, core].reshape(256, HD), ow[:, cols], preferred_element_type=F32
+        ) + jnp.dot(x[:, core].reshape(256, HD), shift[:, cols], preferred_element_type=F32)
+
+    mid = reduce_scatter(net, attention_part, bufs(0)).astype(BF16).astype(F32)
+    m_ref[y, z, c] = rms_scale(mid, gain_ref[...]).astype(BF16)
+    all_gather(net, m_ref)
+    loads[4].wait()
+    loads[5].wait()
+
+    @pl.loop(0, 2)
+    def _(i):
+        rows = m_ref[pl.ds(2 * i, 2)].reshape(256, D)
+        gate = jnp.dot(rows, gw[...], preferred_element_type=F32)
+        upward = jnp.dot(rows, uw[...], preferred_element_type=F32)
+        hidden[pl.ds(8 * i, 8)] = (jax.nn.gelu(gate, approximate=True) * upward).astype(BF16).reshape(8, 2, 16, 448)
+
+    loads[6].wait()
+
+    def mlp_part(core, k):
+        return jnp.dot(
+            hidden[:, core].reshape(256, 448), dw[:, pl.ds(k * CW, CW)], preferred_element_type=F32
+        )
+
+    total = reduce_scatter(net, mlp_part, bufs(1))
+    out_ref[...] = (mid + total).astype(BF16)
+    net.drain()
+
+
+def post(heads_out, x, shift, out_weight, mlp_gain, gate_weight, up_weight, down_weight):
+    anywhere = pl.BlockSpec(memory_space=pl.ANY)
+    vmem = pl.BlockSpec(memory_space=pltpu.VMEM)
+    copies = 2 * CHUNKS * 10 + 22
+    return pl.pallas_call(
+        post_kernel,
+        out_shape=jax.ShapeDtypeStruct((16, D), BF16),
+        in_specs=[anywhere, anywhere, anywhere, anywhere, vmem, anywhere, anywhere, anywhere],
+        out_specs=vmem,
+        scratch_shapes=[
+            pltpu.VMEM((16, 2, 16, HD), BF16),
+            pltpu.VMEM((16, 2, 16, HD), BF16),
+            pltpu.VMEM((HD, D), BF16),
+            pltpu.VMEM((HD, D), BF16),
+            pltpu.VMEM((D, 448), BF16),
+            pltpu.VMEM((D, 448), BF16),
+            pltpu.VMEM((448, D), BF16),
+            pltpu.VMEM((4, 4, 2, 16, D), BF16),
+            pltpu.VMEM((16, 2, 16, 448), BF16),
+            pltpu.VMEM((2, CHUNKS, 256, CW), BF16),
+            pltpu.VMEM((2, CHUNKS, 256, CW), BF16),
+            pltpu.VMEM((2, CHUNKS, 4, 4, 16, CW), BF16),
+            pltpu.VMEM((2, CHUNKS, 2, 2, 16, CW), BF16),
+            pltpu.VMEM((2, CHUNKS, 2, 4, 16, CW), BF16),
+            pltpu.VMEM((2, CHUNKS, 4, 16, CW), BF16),
+            pltpu.VMEM((2, CHUNKS, 3, 16, CW), BF16),
+            pltpu.SemaphoreType.DMA((copies,)),
+            pltpu.SemaphoreType.DMA((copies,)),
+            pltpu.SemaphoreType.DMA((7,)),
+        ],
+        compiler_params=pltpu.CompilerParams(
+            collective_id=1, has_side_effects=True, vmem_limit_bytes=58 * 1024 * 1024
+        ),
+        name="post_attention",
+    )(
+        heads_out.reshape(16, 2, 16, HD), x.reshape(16, 2, 16, HD), shift, out_weight,
+        mlp_gain.reshape(1, D), gate_weight, up_weight, down_weight,
+    )
 
 
 def rotate(values, position):
@@ -40,17 +315,8 @@
 
 
 def shards(
-    layer_input,
-    norm_gain,
-    qkv_weight,
-    cache_keys,
-    cache_values,
-    cache_lengths,
-    out_weight,
-    mlp_gain,
-    gate_weight,
-    up_weight,
-    down_weight,
+    layer_input, norm_gain, qkv_weight, cache_keys, cache_values, cache_lengths,
+    out_weight, mlp_gain, gate_weight, up_weight, down_weight,
 ):
     span = layer_input.shape[0]
     heads_dev = cache_keys.shape[2] // HD
@@ -58,9 +324,8 @@
     scale = HD ** (-0.5)
     whole_input = lax.all_gather(layer_input, "hid", axis=1, tiled=True)
     normed = rms_scale(whole_input.astype(jnp.float32), norm_gain).astype(jnp.bfloat16)
-    columns = normed
     projected = jnp.dot(
-        columns,
+        normed,
         lax.all_gather(qkv_weight, "req", axis=0, tiled=True),
         preferred_element_type=jnp.float32,
     ).reshape(span, heads_dev, 3, HD)
@@ -97,25 +362,11 @@
     fresh_scores = jnp.where(causal[None, :, :], fresh_scores, -1e30)
     top, total, accum = merge_block(state, fresh_scores, fresh_values)
     heads_out = (accum / total.T[:, :, None]).astype(jnp.bfloat16).reshape(span, heads_dev * HD)
-    row_count = span // lax.axis_size("hid")
-    row_start = lax.axis_index("hid") * row_count
-    attention = lax.psum(
-        jnp.dot(heads_out, out_weight, preferred_element_type=jnp.float32).astype(jnp.bfloat16),
-        "hid",
-    ).astype(jnp.float32)
-    mid = (whole_input[:, :D].astype(jnp.float32) + attention).astype(jnp.bfloat16)
-    mlp_in = rms_scale(mid.astype(jnp.float32), mlp_gain).astype(jnp.bfloat16)
-    gate = jnp.dot(mlp_in, gate_weight, preferred_element_type=jnp.float32)
-    upward = jnp.dot(mlp_in, up_weight, preferred_element_type=jnp.float32)
-    hidden = (jax.nn.gelu(gate, approximate=True) * upward).astype(jnp.bfloat16)
-    mlp_part = lax.psum_scatter(
-        jnp.dot(hidden, down_weight, preferred_element_type=jnp.float32).astype(jnp.bfloat16),
-        "hid",
-        scatter_dimension=0,
-        tiled=True,
-    ).astype(jnp.float32)
-    mid_own = lax.dynamic_slice_in_dim(mid, row_start, row_count, 0)
-    return (mid_own.astype(jnp.float32) + mlp_part).astype(jnp.bfloat16)
+    start = lax.axis_index("hid") * HD
+    shift = (
+        jnp.arange(D, dtype=jnp.int32)[None, :] == start + jnp.arange(HD, dtype=jnp.int32)[:, None]
+    ).astype(BF16)
+    return post(heads_out, layer_input, shift, out_weight, mlp_gain, gate_weight, up_weight, down_weight)
 
 
 def solution(mesh):

time: 437 us -> 275 us (0.63)
  waiting for transfers between devices: 336 us -> 131 us
  Pallas kernels: 0 us -> 65.2 us
  matrix products: 52.2 us -> 33.3 us
  other arithmetic: 19 us -> 14.5 us
    psum x1 -> x0, waiting for transfers between devices: 110 us -> none  [shards(): lax.psum(jnp.dot(heads_out, out_weight, preferred_element_type=jnp.float3...]
    reduce_scatter x1 -> x0, waiting for transfers between devices: 81.4 us -> none  [shards(): lax.psum_scatter(jnp.dot(hidden, down_weight, preferred_element_type=jnp....]
    pallas_call x0 -> x1, Pallas kernels: none -> 65.2 us  [post(): pl.pallas_call(post_kernel, out_shape=jax.ShapeDtypeStruct((16, D), BF16)...]
    dot_general x4 -> x1, matrix products: 28.4 us -> 11 us  [shards(): jnp.dot(normed, lax.all_gather(qkv_weight, 'req', axis=0, tiled=True), pr...]
    all_gather x1, waiting for transfers between devices: 54.1 us -> 39.9 us  [shards(): whole_input = lax.all_gather(layer_input, 'hid', axis=1, tiled=True)]
    reduce_sum x2 -> x1, other arithmetic: 9.55 us -> 4.65 us  [rms_scale(): jnp.mean(values * values, axis=-1, keepdims=True) + epsilon]
    unnamed x15 -> x8, local copies, waits for them, and re-layouts: 8.73 us -> 12.9 us
    dot_general x6 -> x9, matrix products: 14 us -> 11.6 us  [merge_block(): jnp.einsum('hqk,khd->qhd', weights.astype(jnp.bfloat16), values, preferre...]
  transfers between devices with their start and end apart: 4 -> 2, of which waited for: 4 -> 2; matrix products, arithmetic and copies ran while one was open for 3% -> 7% of each run, Pallas kernels for 0% -> 0%
where the time goes in v1:
time: 275 us; the launch traced here: 274 us
  waiting for transfers between devices  131 us (48%)
  Pallas kernels  65.2 us (24%)
  matrix products  33.3 us (12%)
  local copies, waits for them, and re-layouts  15.2 us (6%)
  other arithmetic  14.5 us (5%)
  between operations  14.1 us (5%)
    all_gather x1, waiting for transfers between devices, shards(): lax.all_gather(qkv_weight, 'req', axis=0, tiled=True)  89.6 us
    pallas_call x1, Pallas kernels, post(): pl.pallas_call(post_kernel, out_shape=jax.ShapeDtypeStruct((16, D), BF16)...  65.2 us
    all_gather x1, waiting for transfers between devices, shards(): whole_input = lax.all_gather(layer_input, 'hid', axis=1, tiled=True)  39.9 us
    unnamed x8, local copies, waits for them, and re-layouts  12.9 us
    dot_general x9, matrix products, merge_block(): jnp.einsum('hqk,khd->qhd', weights.astype(jnp.bfloat16), values, preferre...  11.6 us
    dot_general x1, matrix products, shards(): jnp.dot(normed, lax.all_gather(qkv_weight, 'req', axis=0, tiled=True), pr...  11 us
    dot_general x8, matrix products, visit(): jnp.einsum('qhd,khd->hqk', query, keys, preferred_element_type=jnp.float32)  10.3 us
  transfers between devices with their start and end apart: 2, of which 2 were waited for; matrix products, arithmetic and copies ran while one was open for 7% of the time, Pallas kernels for 0%

profile of v1, /device:TPU:2, one launch (start us, length us, event | category | flops | bytes accessed | tf_op | source)
XLA Modules:
  0.0 273.9 jit_solution(17351421151751595609)
XLA Ops:
  8.7 1.8 copy.23
  10.5 1.3 reshape.234.gain_ref
  11.8 5.9 %copy.24.gw_hbm = bf16[3584,448]{1,0:T(8,128)(2,1)} copy(bf16[3584,448]{0,1:T(8,128)(2,1)} %param.21) | data formatting | bytes 6422528 | tf_op args[8]
  17.7 3.6 %copy.25.uw_hbm = bf16[3584,448]{1,0:T(8,128)(2,1)} copy(bf16[3584,448]{0,1:T(8,128)(2,1)S(1)} %copy-done) | data formatting | bytes 6422528 | tf_op args[9]
  21.3 1.6 fusion.20.shift_hbm
  23.0 39.9 %all-gather.3.cloned.1.call-done = bf16[512,7168]{0,1:T(8,128)(2,1)} async-done(((bf16[512,224]{0,1:T(8,128)(2,1)}), bf16[512,7168]{0,1:T(8,128)(2,1)}) %all-gather.3.cloned.1.call-update) | async-done | bytes 7340048 | tf_op jit(solution)/shard_map/all_gather | solution.py:325
  62.9 4.7 %fusion.13 = f32[512]{0:T(512)S(1)} fusion(bf16[512,7168]{0,1:T(8,128)(2,1)} %all-gather.3.cloned.1.call-done), kind=kLoop, calls=%fused_computation.20 | loop fusion | flops 11009536 | bytes 7342080 | tf_op jit(solution)/shard_map/reduce_sum | solution.py:20
  67.6 89.6 %all-gather.5.cloned.1.call-done = bf16[7168,672]{0,1:T(8,128)(2,1)} async-done(((bf16[1792,672]{0,1:T(8,128)(2,1)}), bf16[7168,672]{0,1:T(8,128)(2,1)}) %all-gather.5.cloned.1.call-update) | async-done | bytes 9633808 | tf_op jit(solution)/shard_map/all_gather | solution.py:329
  157.2 11.0 %fusion.16 = f32[512,672]{0,1:T(8,128)S(1)} fusion(bf16[7168,672]{0,1:T(8,128)(2,1)} %all-gather.5.cloned.1.call-done, bf16[512,7168]{0,1:T(8,128)(2,1)} %all-gather.3.cloned.1.call-done, f32[7168]{0:T(1024)S(1)} %copy-done.1, f32[512]{0:T(512)S(1)} %add_rsqrt_fusion), kind=kOutput, calls=%fused_computation.23 | convolution fusion | flops 4947181568 | bytes 18380800 | tf_op jit(solution)/shard_map/dot_general | solution.py:327
  169.4 29.2 %while.14 = (s32[]{:T(128)}, f32[1,512]{1,0:T(1,128)S(1)}, f32[1,512]{1,0:T(1,128)S(1)}, f32[512,1,224]{0,2,1:T(8,128)S(1)}, s32[]{:T(128)}, /*index=5*/s32[]{:T...) while((s32[]{:T(128)}, f32[1,512]{1,0:T(1,128)S(1)}, ...), condition=%wide.region_4.5_spmd, body=%wide.region_1.4_spmd.sunk | while | flops 236947456 | bytes 4785347 | solution.py:355
  171.6 1.4 fusion.68
  173.7 1.3 fusion.66
  175.2 1.4 fusion.68
  178.8 1.4 fusion.68
  180.9 1.3 fusion.66
  182.4 1.4 fusion.68
  186.1 1.4 fusion.68
  188.1 1.3 fusion.66
  189.7 1.4 fusion.68
  193.3 1.4 fusion.68
  195.4 1.3 fusion.66
  196.9 1.4 fusion.68
  200.3 65.2 %post_attention.1 = bf16[16,3584]{1,0:T(8,128)(2,1)} custom-call(bf16[16,2,16,224]{3,2,1,0:T(8,128)(2,1)} %bitcast.79, bf16[16,2,16,224]{3,2,1,0:T(8,128)(2,1)} %bitcast.78, bf16[224,3584]{1,0:T(8,128)(2,1)} %fusion.20.shift_hbm, bf16[224,3584]{1,0:T(8,128)(2,1)} %ow_hbm.1, f32[1,3584]{1,0:T(1,128)} %reshape.234.gain_ref, bf16[3584,448]{1,0:T(8,128)(2,1)} %copy.24.gw_hbm, ...), custom_call_target="tpu_custom_call" | custom-call | tf_op jit(solution)/shard_map/post_attention/pallas_call | solution.py:256
  265.5 1.6 copy.40
  (68 shorter events, 16.5 us)
Async XLA Ops:
  6.5 56.4 %all-gather.3.cloned.1.call-start = ((), (), s32[]{:S(2)}) async-start(), calls=%async_computation | async-start | bytes 7569408 | tf_op jit(solution)/shard_map/all_gather | solution.py:325
  7.3 149.9 %all-gather.5.cloned.1.call-start = ((), (), s32[]{:S(2)}) async-start(), calls=%async_computation.1 | async-start | bytes 12042240 | tf_op jit(solution)/shard_map/all_gather | solution.py:329
  11.8 5.9 %copy-start = (bf16[3584,448]{0,1:T(8,128)(2,1)S(1)}, bf16[3584,448]{0,1:T(8,128)(2,1)}, u32[]{:S(2)}) copy-start(bf16[3584,448]{0,1:T(8,128)(2,1)} %param.22) | copy-start | bytes 9633796
  23.0 134.2 %copy-start.1 = (f32[7168]{0:T(1024)S(1)}, f32[7168]{0:T(1024)}, u32[]{:S(2)}) copy-start(f32[7168]{0:T(1024)} %param.14) | copy-start | bytes 86020
Sparse Core Ops, SparseCore 0:
  9.6 53.2 all-gather.2
  64.6 92.5 all-gather.4
